TPU v7x, 32 devices: a whole 2x2x4 slice. The times are simulated.
32 devices in a mesh: groups: 2 (over x), track: 4 (over y, core), frame: 4 (over z).
Axes of the slice: x: 2, y: 2, z: 4, core: 2. Of those that a mesh axis runs over, the one named last changes fastest.
Arguments:
- frames: bfloat16 [16, 4096, 256], P(('groups', 'frame')), parts along dimension 0, may hold values from -9 to 9
- query_frame: int32 [1024], P(('groups', 'track')), parts along dimension 0, may hold values from 0 to 7
- query_pixel: int32 [1024], P(('groups', 'track')), parts along dimension 0, may hold values from 0 to 4095
- cotangent: float32 [2, 16, 512], P(None, ('groups', 'frame'), 'track'), parts along dimension 1, may hold values from -48 to 48
Outputs:
- frame_grad: float32 [4096, 16, 256], P('track', ('groups', 'frame')), parts along dimension 1
- query_grad: float32 [1024, 256], P(('groups', 'track', 'frame')), parts along dimension 0
There are 2 independent parts, one for each index of `groups`. A program takes and returns all parts, laid end to end along the dimension named above; each array names one. Nothing has to cross between parts.
All inputs are finite; a program needn't handle non-finite values.
Results may differ from a plain program's by a relative error of at most 0.0029.
Values may be sent and summed in bfloat16 or wider, within the bound.
No kernel may reach another device: no remote copies, remote signals or barrier semaphores. Data moves between devices by JAX's collectives and lax.ppermute only.
A program may use at most 64 MiB of HBM per device.

v0:
```python
import functools
import math

import jax
import jax.numpy as jnp
from jax import lax
from jax.experimental import pallas as pl
from jax.experimental.pallas import tpu as pltpu
from jax.sharding import PartitionSpec as P


C = 256
FEAT_H = 64
FEAT_W = 64
LANES = 128
ROW_TILE = 16
LOG2E = math.log2(math.e)
F32 = jnp.float32
BF16 = jnp.bfloat16

COPY_ROWS = 1024
PICK_COLS = 1024
PIXEL_ROWS = 256
BLOCK_ROWS = 8
STEPS = 4
FLIP_ROWS = 256
NT = (((1,), (1,)), ((), ()))
VMEM_SPEC = pl.BlockSpec(memory_space=pltpu.VMEM)
HBM_SPEC = pl.BlockSpec(memory_space=pltpu.HBM)
SMEM_SPEC = pl.BlockSpec(memory_space=pltpu.SMEM)
PARAMS = pltpu.CompilerParams(vmem_limit_bytes=40 << 20)


def xor_permute(value, axis, size, distance):
    return lax.ppermute(value, axis, [(i, i ^ distance) for i in range(size)])


def column_tile(row):
    return jnp.transpose(jnp.broadcast_to(row, (LANES, row.shape[1])))


def pack_stats(stats, channels):
    high = stats.astype(BF16)
    rest = stats - high.astype(F32)
    middle = rest.astype(BF16)
    low = (rest - middle.astype(F32)).astype(BF16)
    pieces = jnp.concatenate([high.astype(F32), middle.astype(F32), low.astype(F32)], axis=0)
    wide = []
    for at in range(0, stats.shape[1], LANES):
        wide.append(pieces[:, at : at + LANES])
    pieces = jnp.concatenate(wide, axis=0)
    rows = -(-pieces.shape[0] // ROW_TILE) * ROW_TILE
    if rows > pieces.shape[0]:
        pieces = jnp.concatenate([pieces, jnp.zeros((rows - pieces.shape[0], LANES), F32)], axis=0)
    return jnp.concatenate([pieces, jnp.zeros((rows, channels - LANES), F32)], axis=1).astype(BF16)


def unpack_stats(rows, count, tracks):
    rows = rows[:, :LANES].astype(F32)
    result = []
    for i in range(tracks // LANES):
        first = 3 * count * i
        high, middle, low = (rows[first + k * count : first + (k + 1) * count] for k in range(3))
        result.append((high + middle) + low)
    return result


def stat_rows_of(held, tracks):
    return -(-3 * 4 * held * (tracks // LANES) // ROW_TILE) * ROW_TILE


def pick_kernel(held, pixels, place, frame_hbm, pixel_hbm, frames_hbm, frames_out, picked_ref, queries, sems):
    rows = held * pixels
    count = rows // COPY_ROWS
    lookups = [
        pltpu.make_async_copy(ref, queries.at[pl.ds(i, 1), :], sems.at[count + i])
        for i, ref in enumerate((frame_hbm, pixel_hbm))
    ]
    for copy in lookups:
        copy.start()
    copies = [
        pltpu.make_async_copy(
            frames_hbm.at[pl.ds(i * COPY_ROWS, COPY_ROWS), :],
            frames_out.at[pl.ds(i * COPY_ROWS, COPY_ROWS), :],
            sems.at[i],
        )
        for i in range(count)
    ]
    for copy in copies:
        copy.start()
    for copy in lookups:
        copy.wait()
    local = queries[0:1, :] - place[0] * held
    inside = (local >= 0) & (local < held)
    index = jnp.where(inside, local * pixels + queries[1:2, :], -1)
    tracks = index.shape[1]
    column = column_tile(index)
    lane = lax.broadcasted_iota(jnp.int32, (tracks, LANES), 1)
    total = jnp.zeros((tracks, picked_ref.shape[1]), F32)
    for i, copy in enumerate(copies):
        copy.wait()
        for start in range(i * COPY_ROWS, (i + 1) * COPY_ROWS, PICK_COLS):
            hits = [
                jnp.where(column - (start + at) == lane, 1.0, 0.0).astype(BF16)
                for at in range(0, PICK_COLS, LANES)
            ]
            total += jnp.dot(
                jnp.concatenate(hits, axis=1),
                frames_out[pl.ds(start, PICK_COLS), :],
                preferred_element_type=F32,
            )
    picked_ref[...] = total.astype(BF16)


def flip_kernel(frames_ref, flipped_ref):
    for start in range(0, frames_ref.shape[0], FLIP_ROWS):
        flipped_ref[:, pl.ds(start, FLIP_ROWS)] = jnp.transpose(frames_ref[pl.ds(start, FLIP_ROWS), :])


def track_kernel(held, pixels, place, parts, feat_ref, frames_ref, flipped_ref, cot_ref, packed_ref, *rest):
    part_refs, rest = rest[: -6 - held], rest[-6 - held :]
    scores, (terms, peaks, sums, ordinals, tables, slopes) = rest[:held], rest[held:]
    tracks = feat_ref.shape[0]
    scale = C ** (-0.5)
    lane = lax.broadcasted_iota(jnp.int32, (1, LANES), 1)
    lane_x = (lane % FEAT_W).astype(F32) * (2.0 / (FEAT_W - 1)) - 1.0
    lane_y = (lane // FEAT_W).astype(F32) * (2.0 / (FEAT_H - 1)) - 1.0
    step_y = (LANES // FEAT_W) * (2.0 / (FEAT_H - 1))
    tiles = pixels // LANES
    width = pixels // STEPS
    height = tracks // STEPS
    feat = feat_ref[...]

    def score_unit(t, step):
        start = step * width
        if not isinstance(step, int):
            start = pl.multiple_of(start, width)
        block = jnp.dot(feat, flipped_ref[:, pl.ds(t * pixels + start, width)], preferred_element_type=F32)
        scores[t][:, pl.ds(start, width)] = block
        peak = peaks[t]
        for at in range(0, width, LANES):
            peak = jnp.maximum(peak, block[:, at : at + LANES])
        peaks[t] = peak

    def peak_unit(t):
        peaks[t] = jnp.broadcast_to(jnp.max(peaks[t], axis=1, keepdims=True) * (scale * LOG2E), (tracks, LANES))

    def soft_unit(t, step):
        for first in range(0, height, BLOCK_ROWS):
            lines = pl.ds(pl.multiple_of(step * height + first, BLOCK_ROWS), BLOCK_ROWS)
            top = peaks[t, lines, :]
            pending, odd = {}, {}
            for tile in range(tiles):
                cols = pl.ds(tile * LANES, LANES)
                value = jnp.exp2(scores[t][lines, cols] * (scale * LOG2E) - top)
                scores[t][lines, cols] = value
                level = 0
                while tile >> level & 1:
                    odd[level] = value if level not in odd else odd[level] + value
                    value = pending.pop(level) + value
                    level += 1
                pending[level] = value
            (total,) = pending.values()
            ordinal = odd[0]
            for level in range(1, len(odd)):
                ordinal = ordinal + odd[level] * float(1 << level)
            sums[lines, :] = total
            ordinals[lines, :] = ordinal

    def table_unit(t):
        total = sums[...]
        gx, gy = (column_tile(cot_ref[k, pl.ds(t, 1), :]) for k in range(2))
        inverse = 1.0 / jnp.sum(total, axis=1, keepdims=True)
        expect_x = jnp.sum(total * lane_x, axis=1, keepdims=True) * inverse
        expect_y = jnp.sum(ordinals[...] * step_y + total * lane_y, axis=1, keepdims=True) * inverse
        factor = inverse * scale
        slopes[...] = gy * (factor * step_y)
        gx, gy, inner = gx * factor, gy * factor, (gx * expect_x + gy * expect_y) * factor
        for value in (peaks[t], gx, gy, inner):
            stat_rows.append(jnp.transpose(value)[0:1])
        tables[...] = gx * lane_x + gy * lane_y - inner

    def grad_unit(t, step):
        table, slope = tables[...], slopes[...]
        half = width // 2
        for k in range(2):
            start = step * width + k * half
            coef = table + slope * (jnp.asarray(step * (width // LANES), F32) + float(k * half // LANES))
            grads = []
            if not isinstance(step, int):
                start = pl.multiple_of(start, half)
            for at in range(0, half, LANES):
                cols = start + at
                cols = cols if isinstance(step, int) else pl.multiple_of(cols, LANES)
                grads.append((scores[t][:, pl.ds(cols, LANES)] * coef).astype(BF16))
                coef = coef + slope
            terms[k] += jnp.dot(
                jnp.concatenate(grads, axis=1),
                frames_ref[pl.ds(t * pixels + start, half), :],
                preferred_element_type=F32,
            )

    stat_rows = []
    terms[...] = jnp.zeros(terms.shape, F32)
    peaks[...] = jnp.full(peaks.shape, -jnp.inf, F32)
    for step in range(STEPS):
        score_unit(0, step)
    for t in range(held):
        peak_unit(t)

        def body(step, carry, t=t):
            if t:
                grad_unit(t - 1, step)
            soft_unit(t, step)
            if t + 1 < held:
                score_unit(t + 1, step)
            return carry

        for step in range(STEPS):
            body(step, 0)
        table_unit(t)
    for step in range(STEPS):
        grad_unit(held - 1, step)
    packed_ref[pl.ds(0, tracks), :] = feat
    packed_ref[pl.ds(tracks, packed_ref.shape[0] - tracks), :] = pack_stats(jnp.concatenate(stat_rows, axis=0), feat.shape[1])
    terms[0] += terms[1]
    share = tracks // parts
    for i, part in enumerate(part_refs):
        owner = place[0] ^ i
        part[...] = terms[0, pl.ds(pl.multiple_of(owner * share, share), share), :]


def frame_kernel(held, pixels, own, tracks, place, block_refs, frames_ref, emit):
    scale = C ** (-0.5)
    start_row = place[1] * own
    image_row0 = (start_row // FEAT_W).astype(F32)
    line_x = (lax.broadcasted_iota(jnp.int32, (FEAT_W, LANES), 0)).astype(F32) * (2.0 / (FEAT_W - 1)) - 1.0
    everyone = jnp.concatenate([ref[pl.ds(0, tracks), :] for ref in block_refs], axis=0)
    stats = []
    for ref in block_refs:
        stats += unpack_stats(ref[pl.ds(tracks, ref.shape[0] - tracks), :], 4 * held, tracks)
    chunk = min(own, PIXEL_ROWS)
    units = [(first, t) for first in range(0, own, chunk) for t in range(held)]

    def score_of(first, t):
        lines = frames_ref[pl.ds(pl.multiple_of(t * pixels + start_row + first, FEAT_W), chunk), :]
        return lax.dot_general(lines, everyone, NT, preferred_element_type=F32) * (scale * LOG2E)

    def grad_of(first, t, score):
        images = []
        for image in range(chunk // FEAT_W):
            coord_y = (image_row0 + (first // FEAT_W + image)) * (2.0 / (FEAT_H - 1)) - 1.0
            grads = []
            for b, stat in enumerate(stats):
                peak, gx, gy, inner = (stat[4 * t + k : 4 * t + k + 1] for k in range(4))
                part = score[image * FEAT_W : (image + 1) * FEAT_W, b * LANES : (b + 1) * LANES]
                power = jnp.exp2(part - peak)
                grads.append((power * (gx * line_x + (gy * coord_y - inner))).astype(BF16))
            images.append(jnp.concatenate(grads, axis=1))
        return jnp.concatenate(images, axis=0)

    for unit in units:
        emit(*unit, jnp.dot(grad_of(*unit, score_of(*unit)), everyone, preferred_element_type=F32))


def pixel_kernel(held, pixels, tracks, place, *refs):
    block_refs, (frames_ref, out_hbm, out, sems) = refs[:-4], refs[-4:]
    lane_tiles = C // LANES
    lines_out = held * lane_tiles
    own = out.shape[0] // lines_out
    copies = []

    def emit(first, t, value):
        chunk = value.shape[0]
        for k in range(lane_tiles):
            out[pl.ds(first * lines_out + k * held + t, chunk, stride=lines_out), :] = value[
                :, k * LANES : (k + 1) * LANES
            ]
        if t == held - 1:
            rows = pl.ds(first * lines_out, chunk * lines_out)
            copy = pltpu.make_async_copy(out.at[rows, :], out_hbm.at[rows, :], sems.at[first // chunk])
            copy.start()
            copies.append(copy)

    frame_kernel(held, pixels, own, tracks, place, block_refs, frames_ref, emit)
    for copy in copies:
        copy.wait()


def on_device(sizes, frames, query_frame, query_pixel, cotangent):
    return steps_on_device(sizes, frames, query_frame, query_pixel, cotangent)


def steps_on_device(sizes, frames, query_frame, query_pixel, cotangent):
    ranks, columns = sizes["frame"], sizes["track"]
    held, pixels, channels = frames.shape
    tracks = query_frame.shape[0]
    place = jnp.stack([lax.axis_index("frame"), lax.axis_index("track")]).astype(jnp.int32)
    frames_hbm, frame_hbm, pixel_hbm = (
        pltpu.with_memory_space_constraint(value, pltpu.HBM)
        for value in (frames.reshape(held * pixels, channels), query_frame[None], query_pixel[None])
    )

    kept, feat = pl.pallas_call(
        functools.partial(pick_kernel, held, pixels),
        out_shape=(pltpu.VMEM((held * pixels, channels), BF16), pltpu.VMEM((tracks, channels), BF16)),
        in_specs=[SMEM_SPEC, HBM_SPEC, HBM_SPEC, HBM_SPEC],
        out_specs=(VMEM_SPEC, VMEM_SPEC),
        scratch_shapes=[
            pltpu.VMEM((2, tracks), jnp.int32),
            pltpu.SemaphoreType.DMA((held * pixels // COPY_ROWS + 2,)),
        ],
        compiler_params=PARAMS,
        name="pick",
    )(place, frame_hbm, pixel_hbm, frames_hbm)

    picks = [feat]
    for i in range(1, ranks):
        picks.append(xor_permute(feat, "frame", ranks, i))
    flipped = pl.pallas_call(
        flip_kernel,
        out_shape=pltpu.VMEM((channels, held * pixels), BF16),
        in_specs=[VMEM_SPEC],
        out_specs=VMEM_SPEC,
        compiler_params=PARAMS,
        cost_estimate=pl.CostEstimate(flops=0, bytes_accessed=4 * held * pixels * channels, transcendentals=0),
        name="flip",
    )(kept)
    feat = sum(picks[1:], picks[0])

    share = tracks // ranks
    packed, *terms = pl.pallas_call(
        lambda place_ref, *refs: track_kernel(held, pixels, place_ref, ranks, *refs),
        out_shape=(pltpu.VMEM((tracks + stat_rows_of(held, tracks), channels), BF16),)
        + tuple(pltpu.VMEM((share, channels), F32) for _ in range(ranks)),
        in_specs=[SMEM_SPEC, VMEM_SPEC, VMEM_SPEC, VMEM_SPEC, VMEM_SPEC],
        out_specs=(VMEM_SPEC,) * (1 + ranks),
        scratch_shapes=[
            *[pltpu.VMEM((tracks, pixels), F32)] * held,
            pltpu.VMEM((2, tracks, channels), F32),
            pltpu.VMEM((held, tracks, LANES), F32),
        ]
        + [pltpu.VMEM((tracks, LANES), F32)] * 4,
        compiler_params=PARAMS,
        name="own_tracks",
    )(place, feat, kept, flipped, cotangent)

    far_blocks, distance = [], columns // 2
    while distance > 1:
        far_blocks += [xor_permute(block, "track", columns, distance) for block in [packed] + far_blocks]
        distance //= 2
    arrived = []
    for i in range(1, ranks):
        arrived.append(xor_permute(terms[i], "frame", ranks, i))
    near_blocks = [packed, xor_permute(packed, "track", columns, 1)]

    own = pixels // columns
    lines_out = held * channels // LANES

    def cost(count):
        return pl.CostEstimate(
            flops=4 * held * own * tracks * count * channels,
            bytes_accessed=4 * held * own * channels,
            transcendentals=held * own * tracks * count,
        )

    far_blocks += [xor_permute(block, "track", columns, 1) for block in far_blocks]
    query_grad = terms[0]

    frame_grad = pl.pallas_call(
        functools.partial(pixel_kernel, held, pixels, tracks),
        out_shape=jax.ShapeDtypeStruct((own * lines_out, LANES), F32),
        in_specs=[SMEM_SPEC] + [VMEM_SPEC] * (columns + 1),
        out_specs=HBM_SPEC,
        scratch_shapes=[
            pltpu.VMEM((own * lines_out, LANES), F32),
            pltpu.SemaphoreType.DMA((own // min(own, PIXEL_ROWS),)),
        ],
        compiler_params=PARAMS,
        cost_estimate=cost(columns),
        name="own_pixels",
    )(place, *near_blocks, *far_blocks, kept)
    frame_grad, query_grad, *arrived = lax.optimization_barrier((frame_grad, query_grad, *arrived))
    frame_grad = frame_grad.reshape(own, channels // LANES, held, LANES)
    frame_grad = jnp.transpose(frame_grad, (0, 2, 1, 3)).reshape(own, held, channels)
    for value in arrived:
        query_grad = query_grad + value
    return (frame_grad, query_grad)


def solution(mesh):
    return jax.shard_map(
        functools.partial(on_device, dict(mesh.shape)),
        mesh=mesh,
        in_specs=(
            P(("groups", "frame"), None, None),
            P(("groups", "track")),
            P(("groups", "track")),
            P(None, ("groups", "frame"), "track"),
        ),
        out_specs=(P("track", ("groups", "frame"), None), P(("groups", "track", "frame"), None)),
        check_vma=False,
    )
```

profile of v0, /device:TPU:0, one launch (start us, length us, event | category | flops | bytes accessed | tf_op | source)
XLA Modules:
  0.0 32.2 jit_solution(13679530783676468299)
XLA Ops:
  0.6 0.1 pad_add_fusion.place.place_ref
  0.7 3.4 %pick.1 = (bf16[8192,256]{1,0:T(8,128)(2,1)S(1)}, bf16[128,256]{1,0:T(8,128)(2,1)S(1)}) custom-call(s32[2]{0:T(128)S(1)} %pad_add_fusion.place.place_ref, s32[1,128]{1,0:T(1,128)} %bitcast.12, s32[1,128]{1,0:T(1,128)} %bitcast.13, bf16[8192,256]{1,0:T(8,128)(2,1)} %bitcast.10), custom_call_target="tpu_custom_call" | custom-call | tf_op jit(solution)/shard_map/pick/pallas_call | solution.py:304
  4.1 5.1 %collective-permute-start.2 = (bf16[128,256]{1,0:T(8,128)(2,1)S(1)}, bf16[128,256]{1,0:T(8,128)(2,1)S(1)}, u32[]{:S(2)}, u32[]{:S(2)}) collective-permute-start(bf16[128,256]{1,0:T(8,128)(2,1)S(1)} %get-tuple-element.14), channel_id=1, source_target_pairs={{0,3},{1,2},{2,1},{3,0},{4,7},{5,6},{6,5},{7,4},{8,11},{9,10},{10,... | collective-permute-start | bytes 196616 | tf_op jit(solution)/shard_map/ppermute | solution.py:35
  9.3 0.0 collective-permute-start.1
  9.3 0.6 %collective-permute-start = (bf16[128,256]{1,0:T(8,128)(2,1)S(1)}, bf16[128,256]{1,0:T(8,128)(2,1)S(1)}, u32[]{:S(2)}, u32[]{:S(2)}) collective-permute-start(bf16[128,256]{1,0:T(8,128)(2,1)S(1)} %get-tuple-element.14), channel_id=1, source_target_pairs={{0,1},{1,0},{2,3},{3,2},{4,5},{5,4},{6,7},{7,6},{8,9},{9,8},{10,11... | collective-permute-start | bytes 196616 | tf_op jit(solution)/shard_map/ppermute | solution.py:35
  9.9 0.0 copy-start
  9.9 1.2 %flip.1.refs_2_ = bf16[256,8192]{1,0:T(8,128)(2,1)S(1)} custom-call(bf16[8192,256]{1,0:T(8,128)(2,1)S(1)} %get-tuple-element.15.frames_ref.refs_1_.refs_4_), custom_call_target="tpu_custom_call" | custom-call | bytes 8388608 | tf_op jit(solution)/shard_map/flip/pallas_call | solution.py:320
  11.1 0.6 %collective-permute-done.2 = bf16[128,256]{1,0:T(8,128)(2,1)S(1)} collective-permute-done((bf16[128,256]{1,0:T(8,128)(2,1)S(1)}, bf16[128,256]{1,0:T(8,128)(2,1)S(1)}, u32[]{:S(2)}, u32[]{:S(2)}) %collective-permute-start.2) | collective-permute-done | bytes 65568 | tf_op jit(solution)/shard_map/ppermute | solution.py:35
  11.8 3.1 %collective-permute-done.1 = bf16[128,256]{1,0:T(8,128)(2,1)S(1)} collective-permute-done((bf16[128,256]{1,0:T(8,128)(2,1)S(1)}, bf16[128,256]{1,0:T(8,128)(2,1)S(1)}, u32[]{:S(2)}, u32[]{:S(2)}) %collective-permute-start.1) | collective-permute-done | bytes 65568 | tf_op jit(solution)/shard_map/ppermute | solution.py:35
  14.9 0.0 collective-permute-done
  14.9 0.0 copy-done
  14.9 3.2 %own_tracks.1 = (bf16[160,256]{1,0:T(8,128)(2,1)S(1)}, f32[32,256]{1,0:T(8,128)S(1)}, f32[32,256]{1,0:T(8,128)S(1)}, f32[32,256]{1,0:T(8,128)S(1)}, f32[32,256]{1,0:T(8,128)S(1)}) custom-call(s32[2]{0:T(128)S(1)} %pad_add_fusion.place.place_ref, bf16[128,256]{1,0:T(8,128)(2,1)S(1)} %add_add_fusion.refs_0_, ...), custom_call_target="tpu_custom_call" | custom-call | tf_op jit(solution)/shard_map/own_tracks/pallas_call | solution.py:332
  18.1 1.6 %collective-permute-start.4 = (bf16[160,256]{1,0:T(8,128)(2,1)S(1)}, bf16[160,256]{1,0:T(8,128)(2,1)S(1)}, u32[]{:S(2)}, u32[]{:S(2)}) collective-permute-start(bf16[160,256]{1,0:T(8,128)(2,1)S(1)} %get-tuple-element.16.refs_0_), channel_id=1, source_target_pairs={{0,8},{4,12},{8,0},{12,4},{1,9},{5,13},{9,1},{13,5},{2,10},{6,14},... | collective-permute-start | bytes 245768 | tf_op jit(solution)/shard_map/ppermute | solution.py:35
  19.7 0.0 collective-permute-start.3
  19.7 2.9 %collective-permute-done.4.refs_2_ = bf16[160,256]{1,0:T(8,128)(2,1)S(1)} collective-permute-done((bf16[160,256]{1,0:T(8,128)(2,1)S(1)}, bf16[160,256]{1,0:T(8,128)(2,1)S(1)}, u32[]{:S(2)}, u32[]{:S(2)}) %collective-permute-start.4) | collective-permute-done | bytes 81952 | tf_op jit(solution)/shard_map/ppermute | solution.py:35
  22.6 0.0 collective-permute-start.5
  22.6 1.1 %collective-permute-start.6 = (f32[32,256]{1,0:T(8,128)S(1)}, f32[32,256]{1,0:T(8,128)S(1)}, u32[]{:S(2)}, u32[]{:S(2)}) collective-permute-start(f32[32,256]{1,0:T(8,128)S(1)} %get-tuple-element.18), channel_id=1, source_target_pairs={{0,1},{1,0},{2,3},{3,2},{4,5},{5,4},{6,7},{7,6},{8,9},{9,8},{10,11... | collective-permute-start | bytes 98312 | tf_op jit(solution)/shard_map/ppermute | solution.py:35
  23.7 2.2 %collective-permute-start.7 = (f32[32,256]{1,0:T(8,128)S(1)}, f32[32,256]{1,0:T(8,128)S(1)}, u32[]{:S(2)}, u32[]{:S(2)}) collective-permute-start(f32[32,256]{1,0:T(8,128)S(1)} %get-tuple-element.19), channel_id=1, source_target_pairs={{0,2},{1,3},{2,0},{3,1},{4,6},{5,7},{6,4},{7,5},{8,10},{9,11},{10,... | collective-permute-start | bytes 98312 | tf_op jit(solution)/shard_map/ppermute | solution.py:35
  25.9 1.1 %collective-permute-start.8 = (f32[32,256]{1,0:T(8,128)S(1)}, f32[32,256]{1,0:T(8,128)S(1)}, u32[]{:S(2)}, u32[]{:S(2)}) collective-permute-start(f32[32,256]{1,0:T(8,128)S(1)} %get-tuple-element.20), channel_id=1, source_target_pairs={{0,3},{1,2},{2,1},{3,0},{4,7},{5,6},{6,5},{7,4},{8,11},{9,10},{10,... | collective-permute-start | bytes 98312 | tf_op jit(solution)/shard_map/ppermute | solution.py:35
  27.0 0.0 collective-permute-done.3.refs_1_
  27.0 0.0 collective-permute-done.5.refs_3_
  27.0 2.8 %own_pixels.1 = f32[4096,128]{1,0:T(8,128)} custom-call(s32[2]{0:T(128)S(1)} %pad_add_fusion.place.place_ref, bf16[160,256]{1,0:T(8,128)(2,1)S(1)} %get-tuple-element.16.refs_0_, bf16[160,256]{1,0:T(8,128)(2,1)S(1)} %collective-permute-done.3.refs_1_, bf16[160,256]{1,0:T(8,128)(2,1)S(1)} %collective-permute-done.4.refs_2_, ...), custom_call_target="tpu_custom_call" | custom-call | flops 1073741824 | bytes 2097152 | tf_op jit(solution)/shard_map/own_pixels/pallas_call | solution.py:370
  29.8 0.0 collective-permute-done.6
  29.8 0.0 collective-permute-done.7
  29.8 1.8 %collective-permute-done.8 = f32[32,256]{1,0:T(8,128)S(1)} collective-permute-done((f32[32,256]{1,0:T(8,128)S(1)}, f32[32,256]{1,0:T(8,128)S(1)}, u32[]{:S(2)}, u32[]{:S(2)}) %collective-permute-start.8) | collective-permute-done | bytes 32800 | tf_op jit(solution)/shard_map/ppermute | solution.py:35
  31.6 0.6 %add_add_fusion.1 = f32[32,256]{1,0:T(8,128)} fusion(f32[32,256]{1,0:T(8,128)S(1)} %collective-permute-done.8, f32[32,256]{1,0:T(8,128)S(1)} %collective-permute-done.7, f32[32,256]{1,0:T(8,128)S(1)} %get-tuple-element.22, f32[32,256]{1,0:T(8,128)S(1)} %collective-permute-done.6), kind=kLoop, calls=%fused_computation.1 | loop fusion | flops 24576 | bytes 163840 | tf_op jit(solution)/shard_map/add | solution.py:387
  (1 shorter events, 0.0 us)
Async XLA Ops:
  4.1 7.6 %collective-permute-start.2 = (bf16[128,256]{1,0:T(8,128)(2,1)S(1)}, bf16[128,256]{1,0:T(8,128)(2,1)S(1)}, u32[]{:S(2)}, u32[]{:S(2)}) collective-permute-start(bf16[128,256]{1,0:T(8,128)(2,1)S(1)} %get-tuple-element.14), channel_id=1, source_target_pairs={{0,3},{1,2},{2,1},{3,0},{4,7},{5,6},{6,5},{7,4},{8,11},{9,10},{10,... | collective-permute-start | bytes 196616 | tf_op jit(solution)/shard_map/ppermute | solution.py:35
  9.3 5.6 %collective-permute-start.1 = (bf16[128,256]{1,0:T(8,128)(2,1)S(1)}, bf16[128,256]{1,0:T(8,128)(2,1)S(1)}, u32[]{:S(2)}, u32[]{:S(2)}) collective-permute-start(bf16[128,256]{1,0:T(8,128)(2,1)S(1)} %get-tuple-element.14), channel_id=1, source_target_pairs={{0,2},{1,3},{2,0},{3,1},{4,6},{5,7},{6,4},{7,5},{8,10},{9,11},{10,... | collective-permute-start | bytes 196616 | tf_op jit(solution)/shard_map/ppermute | solution.py:35
  9.3 5.6 %collective-permute-start = (bf16[128,256]{1,0:T(8,128)(2,1)S(1)}, bf16[128,256]{1,0:T(8,128)(2,1)S(1)}, u32[]{:S(2)}, u32[]{:S(2)}) collective-permute-start(bf16[128,256]{1,0:T(8,128)(2,1)S(1)} %get-tuple-element.14), channel_id=1, source_target_pairs={{0,1},{1,0},{2,3},{3,2},{4,5},{5,4},{6,7},{7,6},{8,9},{9,8},{10,11... | collective-permute-start | bytes 196616 | tf_op jit(solution)/shard_map/ppermute | solution.py:35
  9.9 5.0 %copy-start = (f32[2,2,128]{2,1,0:T(2,128)S(1)}, f32[2,2,128]{2,1,0:T(2,128)}, u32[]{:S(2)}) copy-start(f32[2,2,128]{2,1,0:T(2,128)} %refs_3_.1) | copy-start | bytes 6148
  18.1 4.5 %collective-permute-start.4 = (bf16[160,256]{1,0:T(8,128)(2,1)S(1)}, bf16[160,256]{1,0:T(8,128)(2,1)S(1)}, u32[]{:S(2)}, u32[]{:S(2)}) collective-permute-start(bf16[160,256]{1,0:T(8,128)(2,1)S(1)} %get-tuple-element.16.refs_0_), channel_id=1, source_target_pairs={{0,8},{4,12},{8,0},{12,4},{1,9},{5,13},{9,1},{13,5},{2,10},{6,14},... | collective-permute-start | bytes 245768 | tf_op jit(solution)/shard_map/ppermute | solution.py:35
  19.7 7.3 %collective-permute-start.3 = (bf16[160,256]{1,0:T(8,128)(2,1)S(1)}, bf16[160,256]{1,0:T(8,128)(2,1)S(1)}, u32[]{:S(2)}, u32[]{:S(2)}) collective-permute-start(bf16[160,256]{1,0:T(8,128)(2,1)S(1)} %get-tuple-element.16.refs_0_), channel_id=1, source_target_pairs={{0,4},{4,0},{8,12},{12,8},{1,5},{5,1},{9,13},{13,9},{2,6},{6,2},{1... | collective-permute-start | bytes 245768 | tf_op jit(solution)/shard_map/ppermute | solution.py:35
  22.6 4.4 %collective-permute-start.5 = (bf16[160,256]{1,0:T(8,128)(2,1)S(1)}, bf16[160,256]{1,0:T(8,128)(2,1)S(1)}, u32[]{:S(2)}, u32[]{:S(2)}) collective-permute-start(bf16[160,256]{1,0:T(8,128)(2,1)S(1)} %collective-permute-done.4.refs_2_), channel_id=1, source_target_pairs={{0,4},{4,0},{8,12},{12,8},{1,5},{5,1},{9,13},{13,9},{2,6},{6,2},{1... | collective-permute-start | bytes 245768 | tf_op jit(solution)/shard_map/ppermute | solution.py:35
  22.6 7.2 %collective-permute-start.6 = (f32[32,256]{1,0:T(8,128)S(1)}, f32[32,256]{1,0:T(8,128)S(1)}, u32[]{:S(2)}, u32[]{:S(2)}) collective-permute-start(f32[32,256]{1,0:T(8,128)S(1)} %get-tuple-element.18), channel_id=1, source_target_pairs={{0,1},{1,0},{2,3},{3,2},{4,5},{5,4},{6,7},{7,6},{8,9},{9,8},{10,11... | collective-permute-start | bytes 98312 | tf_op jit(solution)/shard_map/ppermute | solution.py:35
  23.7 6.1 %collective-permute-start.7 = (f32[32,256]{1,0:T(8,128)S(1)}, f32[32,256]{1,0:T(8,128)S(1)}, u32[]{:S(2)}, u32[]{:S(2)}) collective-permute-start(f32[32,256]{1,0:T(8,128)S(1)} %get-tuple-element.19), channel_id=1, source_target_pairs={{0,2},{1,3},{2,0},{3,1},{4,6},{5,7},{6,4},{7,5},{8,10},{9,11},{10,... | collective-permute-start | bytes 98312 | tf_op jit(solution)/shard_map/ppermute | solution.py:35
  25.9 5.7 %collective-permute-start.8 = (f32[32,256]{1,0:T(8,128)S(1)}, f32[32,256]{1,0:T(8,128)S(1)}, u32[]{:S(2)}, u32[]{:S(2)}) collective-permute-start(f32[32,256]{1,0:T(8,128)S(1)} %get-tuple-element.20), channel_id=1, source_target_pairs={{0,3},{1,2},{2,1},{3,0},{4,7},{5,6},{6,5},{7,4},{8,11},{9,10},{10,... | collective-permute-start | bytes 98312 | tf_op jit(solution)/shard_map/ppermute | solution.py:35
where the time goes:
time: 32.4 us; the launch traced here: 32.2 us
  starting transfers between devices  11.8 us (36%)
  Pallas kernels  10.6 us (33%)
  waiting for transfers between devices  8.45 us (26%)
  other arithmetic  0.72 us (2%)
  between operations  0.7 us (2%)
    ppermute x9, starting transfers between devices, xor_permute(): return lax.ppermute(value, axis, [(i, i ^ distance) for i in range(size)])  11.8 us
    ppermute x9, waiting for transfers between devices, xor_permute(): return lax.ppermute(value, axis, [(i, i ^ distance) for i in range(size)])  8.45 us
    pallas_call x1, Pallas kernels, steps_on_device(): pl.pallas_call(functools.partial(pick_kernel, held, pixels), out_shape=(p...  3.41 us
    pallas_call x1, Pallas kernels, steps_on_device(): pl.pallas_call(lambda place_ref, *refs: track_kernel(held, pixels, place_...  3.17 us
    pallas_call x1, Pallas kernels, steps_on_device(): pl.pallas_call(functools.partial(pixel_kernel, held, pixels, tracks), out...  2.8 us
    pallas_call x1, Pallas kernels, steps_on_device(): pl.pallas_call(flip_kernel, out_shape=pltpu.VMEM((channels, held * pixels...  1.21 us
  transfers between devices with their start and end apart: 9, of which 4 were waited for; matrix products, arithmetic and copies ran while one was open for 0% of the time, Pallas kernels for 12%

commit v1 on v0

--- a/solution.py
+++ b/solution.py
@@ -19,10 +19,10 @@
 BF16 = jnp.bfloat16
 
 COPY_ROWS = 1024
-PICK_COLS = 1024
+PICK_COLS = 512
 PIXEL_ROWS = 256
 BLOCK_ROWS = 8
-STEPS = 4
+STEPS = 8
 FLIP_ROWS = 256
 NT = (((1,), (1,)), ((), ()))
 VMEM_SPEC = pl.BlockSpec(memory_space=pltpu.VMEM)
@@ -69,7 +69,7 @@
     return -(-3 * 4 * held * (tracks // LANES) // ROW_TILE) * ROW_TILE
 
 
-def pick_kernel(held, pixels, place, frame_hbm, pixel_hbm, frames_hbm, frames_out, picked_ref, queries, sems):
+def pick_kernel(held, pixels, place, frame_hbm, pixel_hbm, frames_hbm, frames_out, picked_ref, queries, totals, sems):
     rows = held * pixels
     count = rows // COPY_ROWS
     lookups = [
@@ -96,20 +96,20 @@
     tracks = index.shape[1]
     column = column_tile(index)
     lane = lax.broadcasted_iota(jnp.int32, (tracks, LANES), 1)
-    total = jnp.zeros((tracks, picked_ref.shape[1]), F32)
+    totals[...] = jnp.zeros(totals.shape, F32)
     for i, copy in enumerate(copies):
         copy.wait()
-        for start in range(i * COPY_ROWS, (i + 1) * COPY_ROWS, PICK_COLS):
+        for k, start in enumerate(range(i * COPY_ROWS, (i + 1) * COPY_ROWS, PICK_COLS)):
             hits = [
                 jnp.where(column - (start + at) == lane, 1.0, 0.0).astype(BF16)
                 for at in range(0, PICK_COLS, LANES)
             ]
-            total += jnp.dot(
+            totals[k % 2] += jnp.dot(
                 jnp.concatenate(hits, axis=1),
                 frames_out[pl.ds(start, PICK_COLS), :],
                 preferred_element_type=F32,
             )
-    picked_ref[...] = total.astype(BF16)
+    picked_ref[...] = (totals[0] + totals[1]).astype(BF16)
 
 
 def flip_kernel(frames_ref, flipped_ref):
@@ -308,6 +308,7 @@
         out_specs=(VMEM_SPEC, VMEM_SPEC),
         scratch_shapes=[
             pltpu.VMEM((2, tracks), jnp.int32),
+            pltpu.VMEM((2, tracks, channels), F32),
             pltpu.SemaphoreType.DMA((held * pixels // COPY_ROWS + 2,)),
         ],
         compiler_params=PARAMS,

time: 32.4 us -> 32.2 us (level)
  transfers between devices with their start and end apart: 9 -> 9, of which waited for: 4 -> 4; matrix products, arithmetic and copies ran while one was open for 0% -> 0% of each run, Pallas kernels for 12% -> 13%
where the time goes in v1:
time: 32.2 us; the launch traced here: 32 us
  starting transfers between devices  11.8 us (37%)
  Pallas kernels  10.4 us (32%)
  waiting for transfers between devices  8.44 us (26%)
  other arithmetic  0.72 us (2%)
  between operations  0.7 us (2%)
    ppermute x9, starting transfers between devices, xor_permute(): return lax.ppermute(value, axis, [(i, i ^ distance) for i in range(size)])  11.8 us
    ppermute x9, waiting for transfers between devices, xor_permute(): return lax.ppermute(value, axis, [(i, i ^ distance) for i in range(size)])  8.44 us
    pallas_call x1, Pallas kernels, steps_on_device(): pl.pallas_call(functools.partial(pick_kernel, held, pixels), out_shape=(p...  3.29 us
    pallas_call x1, Pallas kernels, steps_on_device(): pl.pallas_call(lambda place_ref, *refs: track_kernel(held, pixels, place_...  3.11 us
    pallas_call x1, Pallas kernels, steps_on_device(): pl.pallas_call(functools.partial(pixel_kernel, held, pixels, tracks), out...  2.8 us
    pallas_call x1, Pallas kernels, steps_on_device(): pl.pallas_call(flip_kernel, out_shape=pltpu.VMEM((channels, held * pixels...  1.21 us
  transfers between devices with their start and end apart: 9, of which 4 were waited for; matrix products, arithmetic and copies ran while one was open for 0% of the time, Pallas kernels for 13%

profile of v1, /device:TPU:0, one launch (start us, length us, event | category | flops | bytes accessed | tf_op | source)
XLA Modules:
  0.0 32.0 jit_solution(4998130092917097974)
XLA Ops:
  0.6 0.1 pad_add_fusion.place.place_ref
  0.7 3.3 %pick.1 = (bf16[8192,256]{1,0:T(8,128)(2,1)S(1)}, bf16[128,256]{1,0:T(8,128)(2,1)S(1)}) custom-call(s32[2]{0:T(128)S(1)} %pad_add_fusion.place.place_ref, s32[1,128]{1,0:T(1,128)} %bitcast.12, s32[1,128]{1,0:T(1,128)} %bitcast.13, bf16[8192,256]{1,0:T(8,128)(2,1)} %bitcast.10), custom_call_target="tpu_custom_call" | custom-call | tf_op jit(solution)/shard_map/pick/pallas_call | solution.py:304
  4.0 5.1 %collective-permute-start.2 = (bf16[128,256]{1,0:T(8,128)(2,1)S(1)}, bf16[128,256]{1,0:T(8,128)(2,1)S(1)}, u32[]{:S(2)}, u32[]{:S(2)}) collective-permute-start(bf16[128,256]{1,0:T(8,128)(2,1)S(1)} %get-tuple-element.14), channel_id=1, source_target_pairs={{0,3},{1,2},{2,1},{3,0},{4,7},{5,6},{6,5},{7,4},{8,11},{9,10},{10,... | collective-permute-start | bytes 196616 | tf_op jit(solution)/shard_map/ppermute | solution.py:35
  9.2 0.0 collective-permute-start.1
  9.2 0.6 %collective-permute-start = (bf16[128,256]{1,0:T(8,128)(2,1)S(1)}, bf16[128,256]{1,0:T(8,128)(2,1)S(1)}, u32[]{:S(2)}, u32[]{:S(2)}) collective-permute-start(bf16[128,256]{1,0:T(8,128)(2,1)S(1)} %get-tuple-element.14), channel_id=1, source_target_pairs={{0,1},{1,0},{2,3},{3,2},{4,5},{5,4},{6,7},{7,6},{8,9},{9,8},{10,11... | collective-permute-start | bytes 196616 | tf_op jit(solution)/shard_map/ppermute | solution.py:35
  9.8 0.0 copy-start
  9.8 1.2 %flip.1.refs_2_ = bf16[256,8192]{1,0:T(8,128)(2,1)S(1)} custom-call(bf16[8192,256]{1,0:T(8,128)(2,1)S(1)} %get-tuple-element.15.frames_ref.refs_1_.refs_4_), custom_call_target="tpu_custom_call" | custom-call | bytes 8388608 | tf_op jit(solution)/shard_map/flip/pallas_call | solution.py:321
  11.0 0.6 %collective-permute-done.2 = bf16[128,256]{1,0:T(8,128)(2,1)S(1)} collective-permute-done((bf16[128,256]{1,0:T(8,128)(2,1)S(1)}, bf16[128,256]{1,0:T(8,128)(2,1)S(1)}, u32[]{:S(2)}, u32[]{:S(2)}) %collective-permute-start.2) | collective-permute-done | bytes 65568 | tf_op jit(solution)/shard_map/ppermute | solution.py:35
  11.6 3.1 %collective-permute-done.1 = bf16[128,256]{1,0:T(8,128)(2,1)S(1)} collective-permute-done((bf16[128,256]{1,0:T(8,128)(2,1)S(1)}, bf16[128,256]{1,0:T(8,128)(2,1)S(1)}, u32[]{:S(2)}, u32[]{:S(2)}) %collective-permute-start.1) | collective-permute-done | bytes 65568 | tf_op jit(solution)/shard_map/ppermute | solution.py:35
  14.8 0.0 collective-permute-done
  14.8 0.0 copy-done
  14.8 3.1 %own_tracks.1 = (bf16[160,256]{1,0:T(8,128)(2,1)S(1)}, f32[32,256]{1,0:T(8,128)S(1)}, f32[32,256]{1,0:T(8,128)S(1)}, f32[32,256]{1,0:T(8,128)S(1)}, f32[32,256]{1,0:T(8,128)S(1)}) custom-call(s32[2]{0:T(128)S(1)} %pad_add_fusion.place.place_ref, bf16[128,256]{1,0:T(8,128)(2,1)S(1)} %add_add_fusion.refs_0_, ...), custom_call_target="tpu_custom_call" | custom-call | tf_op jit(solution)/shard_map/own_tracks/pallas_call | solution.py:333
  17.9 1.6 %collective-permute-start.4 = (bf16[160,256]{1,0:T(8,128)(2,1)S(1)}, bf16[160,256]{1,0:T(8,128)(2,1)S(1)}, u32[]{:S(2)}, u32[]{:S(2)}) collective-permute-start(bf16[160,256]{1,0:T(8,128)(2,1)S(1)} %get-tuple-element.16.refs_0_), channel_id=1, source_target_pairs={{0,8},{4,12},{8,0},{12,4},{1,9},{5,13},{9,1},{13,5},{2,10},{6,14},... | collective-permute-start | bytes 245768 | tf_op jit(solution)/shard_map/ppermute | solution.py:35
  19.5 0.0 collective-permute-start.3
  19.5 2.9 %collective-permute-done.4.refs_2_ = bf16[160,256]{1,0:T(8,128)(2,1)S(1)} collective-permute-done((bf16[160,256]{1,0:T(8,128)(2,1)S(1)}, bf16[160,256]{1,0:T(8,128)(2,1)S(1)}, u32[]{:S(2)}, u32[]{:S(2)}) %collective-permute-start.4) | collective-permute-done | bytes 81952 | tf_op jit(solution)/shard_map/ppermute | solution.py:35
  22.4 0.0 collective-permute-start.5
  22.4 1.1 %collective-permute-start.6 = (f32[32,256]{1,0:T(8,128)S(1)}, f32[32,256]{1,0:T(8,128)S(1)}, u32[]{:S(2)}, u32[]{:S(2)}) collective-permute-start(f32[32,256]{1,0:T(8,128)S(1)} %get-tuple-element.18), channel_id=1, source_target_pairs={{0,1},{1,0},{2,3},{3,2},{4,5},{5,4},{6,7},{7,6},{8,9},{9,8},{10,11... | collective-permute-start | bytes 98312 | tf_op jit(solution)/shard_map/ppermute | solution.py:35
  23.5 2.2 %collective-permute-start.7 = (f32[32,256]{1,0:T(8,128)S(1)}, f32[32,256]{1,0:T(8,128)S(1)}, u32[]{:S(2)}, u32[]{:S(2)}) collective-permute-start(f32[32,256]{1,0:T(8,128)S(1)} %get-tuple-element.19), channel_id=1, source_target_pairs={{0,2},{1,3},{2,0},{3,1},{4,6},{5,7},{6,4},{7,5},{8,10},{9,11},{10,... | collective-permute-start | bytes 98312 | tf_op jit(solution)/shard_map/ppermute | solution.py:35
  25.7 1.1 %collective-permute-start.8 = (f32[32,256]{1,0:T(8,128)S(1)}, f32[32,256]{1,0:T(8,128)S(1)}, u32[]{:S(2)}, u32[]{:S(2)}) collective-permute-start(f32[32,256]{1,0:T(8,128)S(1)} %get-tuple-element.20), channel_id=1, source_target_pairs={{0,3},{1,2},{2,1},{3,0},{4,7},{5,6},{6,5},{7,4},{8,11},{9,10},{10,... | collective-permute-start | bytes 98312 | tf_op jit(solution)/shard_map/ppermute | solution.py:35
  26.8 0.0 collective-permute-done.3.refs_1_
  26.8 0.0 collective-permute-done.5.refs_3_
  26.8 2.8 %own_pixels.1 = f32[4096,128]{1,0:T(8,128)} custom-call(s32[2]{0:T(128)S(1)} %pad_add_fusion.place.place_ref, bf16[160,256]{1,0:T(8,128)(2,1)S(1)} %get-tuple-element.16.refs_0_, bf16[160,256]{1,0:T(8,128)(2,1)S(1)} %collective-permute-done.3.refs_1_, bf16[160,256]{1,0:T(8,128)(2,1)S(1)} %collective-permute-done.4.refs_2_, ...), custom_call_target="tpu_custom_call" | custom-call | flops 1073741824 | bytes 2097152 | tf_op jit(solution)/shard_map/own_pixels/pallas_call | solution.py:371
  29.6 0.0 collective-permute-done.6
  29.6 0.0 collective-permute-done.7
  29.6 1.8 %collective-permute-done.8 = f32[32,256]{1,0:T(8,128)S(1)} collective-permute-done((f32[32,256]{1,0:T(8,128)S(1)}, f32[32,256]{1,0:T(8,128)S(1)}, u32[]{:S(2)}, u32[]{:S(2)}) %collective-permute-start.8) | collective-permute-done | bytes 32800 | tf_op jit(solution)/shard_map/ppermute | solution.py:35
  31.4 0.6 %add_add_fusion.1 = f32[32,256]{1,0:T(8,128)} fusion(f32[32,256]{1,0:T(8,128)S(1)} %collective-permute-done.8, f32[32,256]{1,0:T(8,128)S(1)} %collective-permute-done.7, f32[32,256]{1,0:T(8,128)S(1)} %get-tuple-element.22, f32[32,256]{1,0:T(8,128)S(1)} %collective-permute-done.6), kind=kLoop, calls=%fused_computation.1 | loop fusion | flops 24576 | bytes 163840 | tf_op jit(solution)/shard_map/add | solution.py:388
  (1 shorter events, 0.0 us)
Async XLA Ops:
  4.0 7.6 %collective-permute-start.2 = (bf16[128,256]{1,0:T(8,128)(2,1)S(1)}, bf16[128,256]{1,0:T(8,128)(2,1)S(1)}, u32[]{:S(2)}, u32[]{:S(2)}) collective-permute-start(bf16[128,256]{1,0:T(8,128)(2,1)S(1)} %get-tuple-element.14), channel_id=1, source_target_pairs={{0,3},{1,2},{2,1},{3,0},{4,7},{5,6},{6,5},{7,4},{8,11},{9,10},{10,... | collective-permute-start | bytes 196616 | tf_op jit(solution)/shard_map/ppermute | solution.py:35
  9.2 5.6 %collective-permute-start.1 = (bf16[128,256]{1,0:T(8,128)(2,1)S(1)}, bf16[128,256]{1,0:T(8,128)(2,1)S(1)}, u32[]{:S(2)}, u32[]{:S(2)}) collective-permute-start(bf16[128,256]{1,0:T(8,128)(2,1)S(1)} %get-tuple-element.14), channel_id=1, source_target_pairs={{0,2},{1,3},{2,0},{3,1},{4,6},{5,7},{6,4},{7,5},{8,10},{9,11},{10,... | collective-permute-start | bytes 196616 | tf_op jit(solution)/shard_map/ppermute | solution.py:35
  9.2 5.6 %collective-permute-start = (bf16[128,256]{1,0:T(8,128)(2,1)S(1)}, bf16[128,256]{1,0:T(8,128)(2,1)S(1)}, u32[]{:S(2)}, u32[]{:S(2)}) collective-permute-start(bf16[128,256]{1,0:T(8,128)(2,1)S(1)} %get-tuple-element.14), channel_id=1, source_target_pairs={{0,1},{1,0},{2,3},{3,2},{4,5},{5,4},{6,7},{7,6},{8,9},{9,8},{10,11... | collective-permute-start | bytes 196616 | tf_op jit(solution)/shard_map/ppermute | solution.py:35
  9.8 5.0 %copy-start = (f32[2,2,128]{2,1,0:T(2,128)S(1)}, f32[2,2,128]{2,1,0:T(2,128)}, u32[]{:S(2)}) copy-start(f32[2,2,128]{2,1,0:T(2,128)} %refs_3_.1) | copy-start | bytes 6148
  17.9 4.5 %collective-permute-start.4 = (bf16[160,256]{1,0:T(8,128)(2,1)S(1)}, bf16[160,256]{1,0:T(8,128)(2,1)S(1)}, u32[]{:S(2)}, u32[]{:S(2)}) collective-permute-start(bf16[160,256]{1,0:T(8,128)(2,1)S(1)} %get-tuple-element.16.refs_0_), channel_id=1, source_target_pairs={{0,8},{4,12},{8,0},{12,4},{1,9},{5,13},{9,1},{13,5},{2,10},{6,14},... | collective-permute-start | bytes 245768 | tf_op jit(solution)/shard_map/ppermute | solution.py:35
  19.5 7.3 %collective-permute-start.3 = (bf16[160,256]{1,0:T(8,128)(2,1)S(1)}, bf16[160,256]{1,0:T(8,128)(2,1)S(1)}, u32[]{:S(2)}, u32[]{:S(2)}) collective-permute-start(bf16[160,256]{1,0:T(8,128)(2,1)S(1)} %get-tuple-element.16.refs_0_), channel_id=1, source_target_pairs={{0,4},{4,0},{8,12},{12,8},{1,5},{5,1},{9,13},{13,9},{2,6},{6,2},{1... | collective-permute-start | bytes 245768 | tf_op jit(solution)/shard_map/ppermute | solution.py:35
  22.4 4.4 %collective-permute-start.5 = (bf16[160,256]{1,0:T(8,128)(2,1)S(1)}, bf16[160,256]{1,0:T(8,128)(2,1)S(1)}, u32[]{:S(2)}, u32[]{:S(2)}) collective-permute-start(bf16[160,256]{1,0:T(8,128)(2,1)S(1)} %collective-permute-done.4.refs_2_), channel_id=1, source_target_pairs={{0,4},{4,0},{8,12},{12,8},{1,5},{5,1},{9,13},{13,9},{2,6},{6,2},{1... | collective-permute-start | bytes 245768 | tf_op jit(solution)/shard_map/ppermute | solution.py:35
  22.4 7.2 %collective-permute-start.6 = (f32[32,256]{1,0:T(8,128)S(1)}, f32[32,256]{1,0:T(8,128)S(1)}, u32[]{:S(2)}, u32[]{:S(2)}) collective-permute-start(f32[32,256]{1,0:T(8,128)S(1)} %get-tuple-element.18), channel_id=1, source_target_pairs={{0,1},{1,0},{2,3},{3,2},{4,5},{5,4},{6,7},{7,6},{8,9},{9,8},{10,11... | collective-permute-start | bytes 98312 | tf_op jit(solution)/shard_map/ppermute | solution.py:35
  23.5 6.1 %collective-permute-start.7 = (f32[32,256]{1,0:T(8,128)S(1)}, f32[32,256]{1,0:T(8,128)S(1)}, u32[]{:S(2)}, u32[]{:S(2)}) collective-permute-start(f32[32,256]{1,0:T(8,128)S(1)} %get-tuple-element.19), channel_id=1, source_target_pairs={{0,2},{1,3},{2,0},{3,1},{4,6},{5,7},{6,4},{7,5},{8,10},{9,11},{10,... | collective-permute-start | bytes 98312 | tf_op jit(solution)/shard_map/ppermute | solution.py:35
  25.7 5.7 %collective-permute-start.8 = (f32[32,256]{1,0:T(8,128)S(1)}, f32[32,256]{1,0:T(8,128)S(1)}, u32[]{:S(2)}, u32[]{:S(2)}) collective-permute-start(f32[32,256]{1,0:T(8,128)S(1)} %get-tuple-element.20), channel_id=1, source_target_pairs={{0,3},{1,2},{2,1},{3,0},{4,7},{5,6},{6,5},{7,4},{8,11},{9,10},{10,... | collective-permute-start | bytes 98312 | tf_op jit(solution)/shard_map/ppermute | solution.py:35

commit v2 on v1

--- a/solution.py
+++ b/solution.py
@@ -49,14 +49,16 @@
     for at in range(0, stats.shape[1], LANES):
         wide.append(pieces[:, at : at + LANES])
     pieces = jnp.concatenate(wide, axis=0)
-    rows = -(-pieces.shape[0] // ROW_TILE) * ROW_TILE
+    fold = channels // LANES
+    rows = -(-pieces.shape[0] // (fold * ROW_TILE)) * fold * ROW_TILE
     if rows > pieces.shape[0]:
         pieces = jnp.concatenate([pieces, jnp.zeros((rows - pieces.shape[0], LANES), F32)], axis=0)
-    return jnp.concatenate([pieces, jnp.zeros((rows, channels - LANES), F32)], axis=1).astype(BF16)
+    deep = rows // fold
+    return jnp.concatenate([pieces[k * deep : (k + 1) * deep] for k in range(fold)], axis=1).astype(BF16)
 
 
 def unpack_stats(rows, count, tracks):
-    rows = rows[:, :LANES].astype(F32)
+    rows = jnp.concatenate([rows[:, at : at + LANES].astype(F32) for at in range(0, rows.shape[1], LANES)], axis=0)
     result = []
     for i in range(tracks // LANES):
         first = 3 * count * i
@@ -66,7 +68,7 @@
 
 
 def stat_rows_of(held, tracks):
-    return -(-3 * 4 * held * (tracks // LANES) // ROW_TILE) * ROW_TILE
+    return -(-3 * 4 * held * (tracks // LANES) // (C // LANES * ROW_TILE)) * ROW_TILE
 
 
 def pick_kernel(held, pixels, place, frame_hbm, pixel_hbm, frames_hbm, frames_out, picked_ref, queries, totals, sems):

time: 32.2 us -> 31.9 us (level)
  no operation moved by 1% of the time
where the time goes in v2:
time: 31.9 us; the launch traced here: 31.7 us
  starting transfers between devices  11.8 us (37%)
  Pallas kernels  10.2 us (32%)
  waiting for transfers between devices  8.37 us (26%)
  other arithmetic  0.72 us (2%)
  between operations  0.7 us (2%)
    ppermute x9, starting transfers between devices, xor_permute(): return lax.ppermute(value, axis, [(i, i ^ distance) for i in range(size)])  11.8 us
    ppermute x9, waiting for transfers between devices, xor_permute(): return lax.ppermute(value, axis, [(i, i ^ distance) for i in range(size)])  8.37 us
    pallas_call x1, Pallas kernels, steps_on_device(): pl.pallas_call(functools.partial(pick_kernel, held, pixels), out_shape=(p...  3.29 us
    pallas_call x1, Pallas kernels, steps_on_device(): pl.pallas_call(lambda place_ref, *refs: track_kernel(held, pixels, place_...  2.9 us
    pallas_call x1, Pallas kernels, steps_on_device(): pl.pallas_call(functools.partial(pixel_kernel, held, pixels, tracks), out...  2.78 us
    pallas_call x1, Pallas kernels, steps_on_device(): pl.pallas_call(flip_kernel, out_shape=pltpu.VMEM((channels, held * pixels...  1.21 us
  transfers between devices with their start and end apart: 9, of which 4 were waited for; matrix products, arithmetic and copies ran while one was open for 0% of the time, Pallas kernels for 13%

profile of v2, /device:TPU:0, one launch (start us, length us, event | category | flops | bytes accessed | tf_op | source)
XLA Modules:
  0.0 31.7 jit_solution(13060461530333299595)
XLA Ops:
  0.6 0.1 pad_add_fusion.place.place_ref
  0.7 3.3 %pick.1 = (bf16[8192,256]{1,0:T(8,128)(2,1)S(1)}, bf16[128,256]{1,0:T(8,128)(2,1)S(1)}) custom-call(s32[2]{0:T(128)S(1)} %pad_add_fusion.place.place_ref, s32[1,128]{1,0:T(1,128)} %bitcast.12, s32[1,128]{1,0:T(1,128)} %bitcast.13, bf16[8192,256]{1,0:T(8,128)(2,1)} %bitcast.10), custom_call_target="tpu_custom_call" | custom-call | tf_op jit(solution)/shard_map/pick/pallas_call | solution.py:306
  4.0 5.1 %collective-permute-start.2 = (bf16[128,256]{1,0:T(8,128)(2,1)S(1)}, bf16[128,256]{1,0:T(8,128)(2,1)S(1)}, u32[]{:S(2)}, u32[]{:S(2)}) collective-permute-start(bf16[128,256]{1,0:T(8,128)(2,1)S(1)} %get-tuple-element.14), channel_id=1, source_target_pairs={{0,3},{1,2},{2,1},{3,0},{4,7},{5,6},{6,5},{7,4},{8,11},{9,10},{10,... | collective-permute-start | bytes 196616 | tf_op jit(solution)/shard_map/ppermute | solution.py:35
  9.2 0.0 collective-permute-start.1
  9.2 0.6 %collective-permute-start = (bf16[128,256]{1,0:T(8,128)(2,1)S(1)}, bf16[128,256]{1,0:T(8,128)(2,1)S(1)}, u32[]{:S(2)}, u32[]{:S(2)}) collective-permute-start(bf16[128,256]{1,0:T(8,128)(2,1)S(1)} %get-tuple-element.14), channel_id=1, source_target_pairs={{0,1},{1,0},{2,3},{3,2},{4,5},{5,4},{6,7},{7,6},{8,9},{9,8},{10,11... | collective-permute-start | bytes 196616 | tf_op jit(solution)/shard_map/ppermute | solution.py:35
  9.8 0.0 copy-start
  9.8 1.2 %flip.1.refs_2_ = bf16[256,8192]{1,0:T(8,128)(2,1)S(1)} custom-call(bf16[8192,256]{1,0:T(8,128)(2,1)S(1)} %get-tuple-element.15.frames_ref.refs_1_.refs_4_), custom_call_target="tpu_custom_call" | custom-call | bytes 8388608 | tf_op jit(solution)/shard_map/flip/pallas_call | solution.py:323
  11.0 0.6 %collective-permute-done.2 = bf16[128,256]{1,0:T(8,128)(2,1)S(1)} collective-permute-done((bf16[128,256]{1,0:T(8,128)(2,1)S(1)}, bf16[128,256]{1,0:T(8,128)(2,1)S(1)}, u32[]{:S(2)}, u32[]{:S(2)}) %collective-permute-start.2) | collective-permute-done | bytes 65568 | tf_op jit(solution)/shard_map/ppermute | solution.py:35
  11.6 3.1 %collective-permute-done.1 = bf16[128,256]{1,0:T(8,128)(2,1)S(1)} collective-permute-done((bf16[128,256]{1,0:T(8,128)(2,1)S(1)}, bf16[128,256]{1,0:T(8,128)(2,1)S(1)}, u32[]{:S(2)}, u32[]{:S(2)}) %collective-permute-start.1) | collective-permute-done | bytes 65568 | tf_op jit(solution)/shard_map/ppermute | solution.py:35
  14.8 0.0 collective-permute-done
  14.8 0.0 copy-done
  14.8 2.9 %own_tracks.1 = (bf16[144,256]{1,0:T(8,128)(2,1)S(1)}, f32[32,256]{1,0:T(8,128)S(1)}, f32[32,256]{1,0:T(8,128)S(1)}, f32[32,256]{1,0:T(8,128)S(1)}, f32[32,256]{1,0:T(8,128)S(1)}) custom-call(s32[2]{0:T(128)S(1)} %pad_add_fusion.place.place_ref, bf16[128,256]{1,0:T(8,128)(2,1)S(1)} %add_add_fusion.refs_0_, ...), custom_call_target="tpu_custom_call" | custom-call | tf_op jit(solution)/shard_map/own_tracks/pallas_call | solution.py:335
  17.7 1.6 %collective-permute-start.4 = (bf16[144,256]{1,0:T(8,128)(2,1)S(1)}, bf16[144,256]{1,0:T(8,128)(2,1)S(1)}, u32[]{:S(2)}, u32[]{:S(2)}) collective-permute-start(bf16[144,256]{1,0:T(8,128)(2,1)S(1)} %get-tuple-element.16.refs_0_), channel_id=1, source_target_pairs={{0,8},{4,12},{8,0},{12,4},{1,9},{5,13},{9,1},{13,5},{2,10},{6,14},... | collective-permute-start | bytes 221192 | tf_op jit(solution)/shard_map/ppermute | solution.py:35
  19.3 0.0 collective-permute-start.3
  19.3 2.8 %collective-permute-done.4.refs_2_ = bf16[144,256]{1,0:T(8,128)(2,1)S(1)} collective-permute-done((bf16[144,256]{1,0:T(8,128)(2,1)S(1)}, bf16[144,256]{1,0:T(8,128)(2,1)S(1)}, u32[]{:S(2)}, u32[]{:S(2)}) %collective-permute-start.4) | collective-permute-done | bytes 73760 | tf_op jit(solution)/shard_map/ppermute | solution.py:35
  22.1 0.0 collective-permute-start.5
  22.1 1.1 %collective-permute-start.6 = (f32[32,256]{1,0:T(8,128)S(1)}, f32[32,256]{1,0:T(8,128)S(1)}, u32[]{:S(2)}, u32[]{:S(2)}) collective-permute-start(f32[32,256]{1,0:T(8,128)S(1)} %get-tuple-element.18), channel_id=1, source_target_pairs={{0,1},{1,0},{2,3},{3,2},{4,5},{5,4},{6,7},{7,6},{8,9},{9,8},{10,11... | collective-permute-start | bytes 98312 | tf_op jit(solution)/shard_map/ppermute | solution.py:35
  23.2 2.2 %collective-permute-start.7 = (f32[32,256]{1,0:T(8,128)S(1)}, f32[32,256]{1,0:T(8,128)S(1)}, u32[]{:S(2)}, u32[]{:S(2)}) collective-permute-start(f32[32,256]{1,0:T(8,128)S(1)} %get-tuple-element.19), channel_id=1, source_target_pairs={{0,2},{1,3},{2,0},{3,1},{4,6},{5,7},{6,4},{7,5},{8,10},{9,11},{10,... | collective-permute-start | bytes 98312 | tf_op jit(solution)/shard_map/ppermute | solution.py:35
  25.4 1.1 %collective-permute-start.8 = (f32[32,256]{1,0:T(8,128)S(1)}, f32[32,256]{1,0:T(8,128)S(1)}, u32[]{:S(2)}, u32[]{:S(2)}) collective-permute-start(f32[32,256]{1,0:T(8,128)S(1)} %get-tuple-element.20), channel_id=1, source_target_pairs={{0,3},{1,2},{2,1},{3,0},{4,7},{5,6},{6,5},{7,4},{8,11},{9,10},{10,... | collective-permute-start | bytes 98312 | tf_op jit(solution)/shard_map/ppermute | solution.py:35
  26.5 0.0 collective-permute-done.3.refs_1_
  26.5 0.0 collective-permute-done.5.refs_3_
  26.5 2.8 %own_pixels.1 = f32[4096,128]{1,0:T(8,128)} custom-call(s32[2]{0:T(128)S(1)} %pad_add_fusion.place.place_ref, bf16[144,256]{1,0:T(8,128)(2,1)S(1)} %get-tuple-element.16.refs_0_, bf16[144,256]{1,0:T(8,128)(2,1)S(1)} %collective-permute-done.3.refs_1_, bf16[144,256]{1,0:T(8,128)(2,1)S(1)} %collective-permute-done.4.refs_2_, ...), custom_call_target="tpu_custom_call" | custom-call | flops 1073741824 | bytes 2097152 | tf_op jit(solution)/shard_map/own_pixels/pallas_call | solution.py:373
  29.3 0.0 collective-permute-done.6
  29.3 0.0 collective-permute-done.7
  29.3 1.8 %collective-permute-done.8 = f32[32,256]{1,0:T(8,128)S(1)} collective-permute-done((f32[32,256]{1,0:T(8,128)S(1)}, f32[32,256]{1,0:T(8,128)S(1)}, u32[]{:S(2)}, u32[]{:S(2)}) %collective-permute-start.8) | collective-permute-done | bytes 32800 | tf_op jit(solution)/shard_map/ppermute | solution.py:35
  31.1 0.6 %add_add_fusion.1 = f32[32,256]{1,0:T(8,128)} fusion(f32[32,256]{1,0:T(8,128)S(1)} %collective-permute-done.8, f32[32,256]{1,0:T(8,128)S(1)} %collective-permute-done.7, f32[32,256]{1,0:T(8,128)S(1)} %get-tuple-element.22, f32[32,256]{1,0:T(8,128)S(1)} %collective-permute-done.6), kind=kLoop, calls=%fused_computation.1 | loop fusion | flops 24576 | bytes 163840 | tf_op jit(solution)/shard_map/add | solution.py:390
  (1 shorter events, 0.0 us)
Async XLA Ops:
  4.0 7.6 %collective-permute-start.2 = (bf16[128,256]{1,0:T(8,128)(2,1)S(1)}, bf16[128,256]{1,0:T(8,128)(2,1)S(1)}, u32[]{:S(2)}, u32[]{:S(2)}) collective-permute-start(bf16[128,256]{1,0:T(8,128)(2,1)S(1)} %get-tuple-element.14), channel_id=1, source_target_pairs={{0,3},{1,2},{2,1},{3,0},{4,7},{5,6},{6,5},{7,4},{8,11},{9,10},{10,... | collective-permute-start | bytes 196616 | tf_op jit(solution)/shard_map/ppermute | solution.py:35
  9.2 5.6 %collective-permute-start.1 = (bf16[128,256]{1,0:T(8,128)(2,1)S(1)}, bf16[128,256]{1,0:T(8,128)(2,1)S(1)}, u32[]{:S(2)}, u32[]{:S(2)}) collective-permute-start(bf16[128,256]{1,0:T(8,128)(2,1)S(1)} %get-tuple-element.14), channel_id=1, source_target_pairs={{0,2},{1,3},{2,0},{3,1},{4,6},{5,7},{6,4},{7,5},{8,10},{9,11},{10,... | collective-permute-start | bytes 196616 | tf_op jit(solution)/shard_map/ppermute | solution.py:35
  9.2 5.6 %collective-permute-start = (bf16[128,256]{1,0:T(8,128)(2,1)S(1)}, bf16[128,256]{1,0:T(8,128)(2,1)S(1)}, u32[]{:S(2)}, u32[]{:S(2)}) collective-permute-start(bf16[128,256]{1,0:T(8,128)(2,1)S(1)} %get-tuple-element.14), channel_id=1, source_target_pairs={{0,1},{1,0},{2,3},{3,2},{4,5},{5,4},{6,7},{7,6},{8,9},{9,8},{10,11... | collective-permute-start | bytes 196616 | tf_op jit(solution)/shard_map/ppermute | solution.py:35
  9.8 5.0 %copy-start = (f32[2,2,128]{2,1,0:T(2,128)S(1)}, f32[2,2,128]{2,1,0:T(2,128)}, u32[]{:S(2)}) copy-start(f32[2,2,128]{2,1,0:T(2,128)} %refs_3_.1) | copy-start | bytes 6148
  17.7 4.4 %collective-permute-start.4 = (bf16[144,256]{1,0:T(8,128)(2,1)S(1)}, bf16[144,256]{1,0:T(8,128)(2,1)S(1)}, u32[]{:S(2)}, u32[]{:S(2)}) collective-permute-start(bf16[144,256]{1,0:T(8,128)(2,1)S(1)} %get-tuple-element.16.refs_0_), channel_id=1, source_target_pairs={{0,8},{4,12},{8,0},{12,4},{1,9},{5,13},{9,1},{13,5},{2,10},{6,14},... | collective-permute-start | bytes 221192 | tf_op jit(solution)/shard_map/ppermute | solution.py:35
  19.3 7.2 %collective-permute-start.3 = (bf16[144,256]{1,0:T(8,128)(2,1)S(1)}, bf16[144,256]{1,0:T(8,128)(2,1)S(1)}, u32[]{:S(2)}, u32[]{:S(2)}) collective-permute-start(bf16[144,256]{1,0:T(8,128)(2,1)S(1)} %get-tuple-element.16.refs_0_), channel_id=1, source_target_pairs={{0,4},{4,0},{8,12},{12,8},{1,5},{5,1},{9,13},{13,9},{2,6},{6,2},{1... | collective-permute-start | bytes 221192 | tf_op jit(solution)/shard_map/ppermute | solution.py:35
  22.1 4.4 %collective-permute-start.5 = (bf16[144,256]{1,0:T(8,128)(2,1)S(1)}, bf16[144,256]{1,0:T(8,128)(2,1)S(1)}, u32[]{:S(2)}, u32[]{:S(2)}) collective-permute-start(bf16[144,256]{1,0:T(8,128)(2,1)S(1)} %collective-permute-done.4.refs_2_), channel_id=1, source_target_pairs={{0,4},{4,0},{8,12},{12,8},{1,5},{5,1},{9,13},{13,9},{2,6},{6,2},{1... | collective-permute-start | bytes 221192 | tf_op jit(solution)/shard_map/ppermute | solution.py:35
  22.1 7.2 %collective-permute-start.6 = (f32[32,256]{1,0:T(8,128)S(1)}, f32[32,256]{1,0:T(8,128)S(1)}, u32[]{:S(2)}, u32[]{:S(2)}) collective-permute-start(f32[32,256]{1,0:T(8,128)S(1)} %get-tuple-element.18), channel_id=1, source_target_pairs={{0,1},{1,0},{2,3},{3,2},{4,5},{5,4},{6,7},{7,6},{8,9},{9,8},{10,11... | collective-permute-start | bytes 98312 | tf_op jit(solution)/shard_map/ppermute | solution.py:35
  23.2 6.1 %collective-permute-start.7 = (f32[32,256]{1,0:T(8,128)S(1)}, f32[32,256]{1,0:T(8,128)S(1)}, u32[]{:S(2)}, u32[]{:S(2)}) collective-permute-start(f32[32,256]{1,0:T(8,128)S(1)} %get-tuple-element.19), channel_id=1, source_target_pairs={{0,2},{1,3},{2,0},{3,1},{4,6},{5,7},{6,4},{7,5},{8,10},{9,11},{10,... | collective-permute-start | bytes 98312 | tf_op jit(solution)/shard_map/ppermute | solution.py:35
  25.4 5.7 %collective-permute-start.8 = (f32[32,256]{1,0:T(8,128)S(1)}, f32[32,256]{1,0:T(8,128)S(1)}, u32[]{:S(2)}, u32[]{:S(2)}) collective-permute-start(f32[32,256]{1,0:T(8,128)S(1)} %get-tuple-element.20), channel_id=1, source_target_pairs={{0,3},{1,2},{2,1},{3,0},{4,7},{5,6},{6,5},{7,4},{8,11},{9,10},{10,... | collective-permute-start | bytes 98312 | tf_op jit(solution)/shard_map/ppermute | solution.py:35
